TPU v7x, 32 devices: a whole 2x2x4 slice. The times are simulated.
32 devices in a mesh: groups: 1, expert: 32 (over z, y, x, core).
Axes of the slice: x: 2, y: 2, z: 4, core: 2. Of those that a mesh axis runs over, the one named last changes fastest.
Arguments:
- hidden_rows: bfloat16 [2, 256, 4096], P(None, ('groups', 'expert')), may hold values from -6 to 6
- expert_ids: int32 [2, 256, 8], P(None, ('groups', 'expert')), may hold values from 0 to 15, all different within a row; in each aligned block of 8 rows (0 to 7, 8 to 15, ..., all dimensions but the last counted through in order) at most 8 rows name the same one
- gate_codes: int32 [2, 256, 8], P(None, ('groups', 'expert')), may hold values from 1 to 1023
- gate_weight: bfloat16 [4096, 16384], P(None, 'expert'), may hold values from -0.09375 to 0.09375
- up_weight: bfloat16 [4096, 16384], P(None, 'expert'), may hold values from -0.09375 to 0.09375
- down_weight: bfloat16 [16384, 4096], P('expert'), may hold values from -0.1875 to 0.1875
Outputs:
- combined: bfloat16 [2, 256, 4096], P(None, ('groups', 'expert'))
Inputs may be any that keep to these rules, and one draw needn't show every extreme that they name: `expert_ids`: each row names 8 different experts; in each decode step no expert is named by more than 8 of the rows of one device, a bound that some block reaches.
All inputs are finite; a program needn't handle non-finite values.
Results may differ from a plain program's by a relative error of at most 0.0085.
Values may be sent and summed in bfloat16 or wider, within the bound.
A program may use at most 64 MiB of HBM per device.

v0:
```python
import jax
import jax.numpy as jnp
from jax import lax
from jax.sharding import PartitionSpec as P

route_scale = 2.5


def swapped(value, axis, bit):
    mask = 2**bit
    pairs = [(source, source ^ mask) for source in range(lax.axis_size(axis))]
    return lax.ppermute(value, axis, pairs)


def half_expert(step_rows, gate_half, up_half, down_half):
    gate_value = jnp.dot(step_rows, gate_half, preferred_element_type=jnp.float32)
    up_value = jnp.dot(step_rows, up_half, preferred_element_type=jnp.float32)
    hidden = (jax.nn.silu(gate_value) * up_value).astype(jnp.bfloat16)
    return jnp.dot(hidden, down_half, preferred_element_type=jnp.float32).astype(jnp.bfloat16)


def expert_apply(got_rows, gate_half, up_half, down_half):
    sources = got_rows.shape[0]
    slot_count = got_rows.shape[1]
    feature_count = got_rows.shape[2]
    total_slots = sources * slot_count
    flat_rows = got_rows.reshape(total_slots, feature_count)
    produced = half_expert(flat_rows, gate_half, up_half, down_half)
    return produced.reshape(sources, slot_count, feature_count)


def pick_ranks(route_ids, expert_count):
    pick_total = route_ids.shape[0] * route_ids.shape[1]
    flat_ids = route_ids.reshape(pick_total)
    one_hot = (flat_ids[:, None] == jnp.arange(expert_count, dtype=jnp.int32)[None, :]).astype(
        jnp.int32
    )
    earlier = jnp.cumsum(one_hot, axis=0) - one_hot
    slot_rank = jnp.sum(earlier * one_hot, axis=1)
    return (flat_ids, slot_rank)


def slot_owner(flat_ids, slot_rank, rows_dev, top_count, expert_count, slot_most):
    pick_order = jnp.arange(flat_ids.shape[0], dtype=jnp.int32)
    owner_slot = jnp.full((expert_count * slot_most,), rows_dev, jnp.int32)
    owner_slot = owner_slot.at[flat_ids * slot_most + slot_rank].set(pick_order // top_count)
    return owner_slot.reshape(expert_count, slot_most)


def combine(expert_out, code_block):
    picked = expert_out.astype(jnp.float32).reshape(code_block.shape[0], code_block.shape[1], -1)
    code_rows = code_block.astype(jnp.float32)
    weights = route_scale * code_rows / jnp.sum(code_rows, axis=1, keepdims=True)
    return jnp.sum(weights[:, :, None] * picked, axis=1).astype(jnp.bfloat16)


def shards(hidden_rows, expert_ids, gate_codes, gate_weight, up_weight, down_weight):
    peer_count = lax.axis_size("expert")
    expert_count = peer_count // 2
    micro_count = hidden_rows.shape[0]
    rows_dev = hidden_rows.shape[1]
    feature_count = hidden_rows.shape[2]
    top_count = expert_ids.shape[2]
    slot_most = min(rows_dev, 2 * rows_dev * top_count // expert_count)
    half_slots = slot_most // 2
    combined = []
    for micro_index in range(micro_count):
        step_rows = hidden_rows[micro_index]
        flat_ids, slot_rank = pick_ranks(expert_ids[micro_index], expert_count)
        padded_rows = jnp.concatenate(
            [step_rows, jnp.zeros((1, feature_count), jnp.bfloat16)], axis=0
        )
        owner_slot = slot_owner(flat_ids, slot_rank, rows_dev, top_count, expert_count, slot_most)
        owner_slot = (
            owner_slot.reshape(expert_count, half_slots, 2)
            .transpose(0, 2, 1)
            .reshape(peer_count, half_slots)
        )
        send_rows = padded_rows[owner_slot]
        received = lax.all_to_all(send_rows, "expert", split_axis=0, concat_axis=0, tiled=True)
        own_count = received.shape[1]
        partner_rows = swapped(received, "expert", 0)
        both_rows = jnp.concatenate([received, partner_rows], axis=1)
        produced = expert_apply(both_rows, gate_weight, up_weight, down_weight)
        from_partner = swapped(produced[:, own_count:], "expert", 0)
        summed = (
            produced[:, :own_count].astype(jnp.float32) + from_partner.astype(jnp.float32)
        ).astype(jnp.bfloat16)
        returned = lax.all_to_all(summed, "expert", split_axis=0, concat_axis=0, tiled=True)
        flat_back = returned.reshape(peer_count * half_slots, feature_count)
        expert_out = flat_back[(2 * flat_ids + slot_rank % 2) * half_slots + slot_rank // 2]
        combined.append(combine(expert_out, gate_codes[micro_index]))
    return jnp.stack(combined, axis=0)


def solution(mesh):
    return jax.shard_map(
        shards,
        mesh=mesh,
        in_specs=(
            P(None, ("groups", "expert"), None),
            P(None, ("groups", "expert"), None),
            P(None, ("groups", "expert"), None),
            P(None, "expert"),
            P(None, "expert"),
            P("expert", None),
        ),
        out_specs=P(None, ("groups", "expert"), None),
        check_vma=False,
    )
```

profile of v0, /device:TPU:8, one launch (start us, length us, event | category | flops | bytes accessed | tf_op | source)
XLA Modules:
  0.0 161.4 jit_solution(14777526055622327873)
XLA Ops:
  0.0 0.7 broadcast_multiply_fusion.1
  0.7 0.1 eq.33
  0.8 0.1 fusion.11
  0.9 0.1 reduce_window_sum.17
  1.0 0.2 select_reduce_fusion.1
  1.1 0.1 mul.131
  1.2 0.1 mul.136
  1.3 0.8 scatter_custom_fusion
  2.1 0.2 reshape_reshape.6
  2.3 0.2 copy.9
  2.5 0.1 reshape.420
  2.6 0.9 slice_bitcast_fusion.1
  3.5 1.2 gather_fusion
  4.7 1.2 reshape.419
  6.0 6.0 %all-to-all-start = ((bf16[32,4,4096]{2,1,0:T(4,128)(2,1)}), bf16[32,4,4096]{2,1,0:T(4,128)(2,1)S(1)}, u32[]{:S(2)}, u32[]{:S(2)}) async-start(bf16[32,4,4096]{2,1,0:T(4,128)(2,1)} %reshape.419), calls=%async_computation | async-start | bytes 2097152 | tf_op jit(solution)/shard_map/all_to_all | solution.py:80
  12.0 0.1 eq.37
  12.1 0.1 fusion.10
  12.2 0.1 reduce_window_sum.18
  12.3 0.1 mul.143
  12.4 0.1 mul.148
  12.4 0.2 select_reduce_fusion
  12.7 0.8 scatter_custom_fusion.1
  13.4 0.2 reshape_reshape.7
  13.6 0.2 copy.10
  13.8 0.1 reshape.436
  14.0 1.2 gather_fusion.2
  15.2 1.2 reshape.435
  16.4 20.9 %all-to-all-done = bf16[32,4,4096]{2,1,0:T(4,128)(2,1)S(1)} async-done(((bf16[32,4,4096]{2,1,0:T(4,128)(2,1)}), bf16[32,4,4096]{2,1,0:T(4,128)(2,1)S(1)}, u32[]{:S(2)}, u32[]{:S(2)}) %all-to-all-start) | async-done | bytes 1048608 | tf_op jit(solution)/shard_map/all_to_all | solution.py:80
  37.3 4.6 %all-to-all-start.2 = ((bf16[32,4,4096]{2,1,0:T(4,128)(2,1)}), bf16[32,4,4096]{2,1,0:T(4,128)(2,1)}, u32[]{:S(2)}, u32[]{:S(2)}) async-start(bf16[32,4,4096]{2,1,0:T(4,128)(2,1)} %reshape.435), calls=%async_computation.2 | async-start | bytes 2097152 | tf_op jit(solution)/shard_map/all_to_all | solution.py:80
  41.9 0.2 collective-permute-start
  42.1 25.1 %all-to-all-done.2 = bf16[32,4,4096]{2,1,0:T(4,128)(2,1)} async-done(((bf16[32,4,4096]{2,1,0:T(4,128)(2,1)}), bf16[32,4,4096]{2,1,0:T(4,128)(2,1)}, u32[]{:S(2)}, u32[]{:S(2)}) %all-to-all-start.2) | async-done | bytes 1048608 | tf_op jit(solution)/shard_map/all_to_all | solution.py:80
  67.3 0.1 collective-permute-start.2
  67.4 0.0 collective-permute-done
  67.4 0.0 copy-start.1
  67.4 1.0 copy-done.1
  68.4 4.3 %fusion.4 = f32[256,512]{1,0:T(8,128)} fusion(bf16[4096,512]{1,0:T(8,128)(2,1)} %param.10, bf16[32,4,4096]{2,1,0:T(4,128)(2,1)S(1)} %collective-permute-done, bf16[32,4,4096]{2,1,0:T(4,128)(2,1)S(1)} %all-to-all-done), kind=kOutput, calls=%fused_computation.16 | convolution fusion | flops 1077936128 | bytes 6815744 | tf_op jit(solution)/shard_map/dot_general | solution.py:17
  72.6 6.4 %fusion = bf16[32,8,4096]{2,1,0:T(8,128)(2,1)S(1)} fusion(bf16[512,4096]{1,0:T(8,128)(2,1)} %param.11, f32[256,512]{1,0:T(8,128)} %fusion.4, bf16[4096,512]{1,0:T(8,128)(2,1)} %param.9, bf16[32,4,4096]{2,1,0:T(4,128)(2,1)} %copy-done.1, bf16[32,4,4096]{2,1,0:T(4,128)(2,1)S(1)} %all-to-all-done), kind=kOutput, calls=%fused_computation.8 | convolution fusion | flops 2153512960 | bytes 13107200 | tf_op jit(solution)/shard_map/dot_general | solution.py:19
  79.1 1.6 slice.49
  80.7 0.4 collective-permute-start.1
  81.1 0.0 collective-permute-done.2
  81.1 4.9 %fusion.2 = f32[256,512]{1,0:T(8,128)} fusion(bf16[4096,512]{1,0:T(8,128)(2,1)} %param.10, bf16[32,4,4096]{2,1,0:T(4,128)(2,1)} %collective-permute-done.2, bf16[32,4,4096]{2,1,0:T(4,128)(2,1)} %all-to-all-done.2), kind=kOutput, calls=%fused_computation.14 | convolution fusion | flops 1077936128 | bytes 6815744 | tf_op jit(solution)/shard_map/dot_general | solution.py:17
  86.0 8.1 %fusion.1 = bf16[32,8,4096]{2,1,0:T(8,128)(2,1)} fusion(bf16[512,4096]{1,0:T(8,128)(2,1)} %param.11, f32[256,512]{1,0:T(8,128)} %fusion.2, bf16[4096,512]{1,0:T(8,128)(2,1)} %param.9, bf16[32,4,4096]{2,1,0:T(4,128)(2,1)} %collective-permute-done.2, bf16[32,4,4096]{2,1,0:T(4,128)(2,1)} %all-to-all-done.2), kind=kOutput, calls=%fused_computation.9 | convolution fusion | flops 2153512960 | bytes 13107200 | tf_op jit(solution)/shard_map/dot_general | solution.py:19
  94.1 3.2 %slice.51 = bf16[32,4,4096]{2,1,0:T(4,128)(2,1)} slice(bf16[32,8,4096]{2,1,0:T(8,128)(2,1)} %fusion.1), slice={[0:32], [4:8], [0:4096]} | slice | bytes 2097152 | tf_op jit(solution)/shard_map/slice | solution.py:85
  97.3 0.1 collective-permute-start.3
  97.4 0.0 collective-permute-done.1
  97.4 1.6 %add_convert_fusion.1 = bf16[32,4,4096]{2,1,0:T(4,128)(2,1)} fusion(bf16[32,4,4096]{2,1,0:T(4,128)(2,1)S(1)} %collective-permute-done.1, bf16[32,8,4096]{2,1,0:T(8,128)(2,1)S(1)} %fusion), kind=kLoop, calls=%fused_computation.13 | loop fusion | flops 2097152 | bytes 3145728 | tf_op jit(solution)/shard_map/convert_element_type | solution.py:88
  99.0 0.0 copy-start
  99.0 4.5 %all-to-all-start.1 = ((bf16[32,4,4096]{2,1,0:T(4,128)(2,1)}), bf16[32,4,4096]{2,1,0:T(4,128)(2,1)S(1)}, u32[]{:S(2)}, u32[]{:S(2)}) async-start(bf16[32,4,4096]{2,1,0:T(4,128)(2,1)} %add_convert_fusion.1), calls=%async_computation.1 | async-start | bytes 2097152 | tf_op jit(solution)/shard_map/all_to_all | solution.py:89
  103.6 0.0 collective-permute-done.3
  103.6 3.7 %add_convert_fusion = bf16[32,4,4096]{2,1,0:T(4,128)(2,1)} fusion(bf16[32,4,4096]{2,1,0:T(4,128)(2,1)} %collective-permute-done.3, bf16[32,8,4096]{2,1,0:T(8,128)(2,1)} %fusion.1), kind=kLoop, calls=%fused_computation.12 | loop fusion | flops 2097152 | bytes 3145728 | tf_op jit(solution)/shard_map/convert_element_type | solution.py:88
  107.3 21.6 %all-to-all-done.1 = bf16[32,4,4096]{2,1,0:T(4,128)(2,1)S(1)} async-done(((bf16[32,4,4096]{2,1,0:T(4,128)(2,1)}), bf16[32,4,4096]{2,1,0:T(4,128)(2,1)S(1)}, u32[]{:S(2)}, u32[]{:S(2)}) %all-to-all-start.1) | async-done | bytes 1048608 | tf_op jit(solution)/shard_map/all_to_all | solution.py:89
  128.9 4.5 %all-to-all-start.3 = ((bf16[32,4,4096]{2,1,0:T(4,128)(2,1)}), bf16[32,4,4096]{2,1,0:T(4,128)(2,1)S(1)}, u32[]{:S(2)}, u32[]{:S(2)}) async-start(bf16[32,4,4096]{2,1,0:T(4,128)(2,1)} %add_convert_fusion), calls=%async_computation.3 | async-start | bytes 2097152 | tf_op jit(solution)/shard_map/all_to_all | solution.py:89
  133.4 0.0 copy-done
  133.5 0.1 convert_reduce_fusion.1
  133.6 0.1 bitcast_divide_fusion.1
  133.7 0.3 reshape.411
  134.0 0.9 gather_fusion.1
  134.8 23.9 %all-to-all-done.3 = bf16[32,4,4096]{2,1,0:T(4,128)(2,1)S(1)} async-done(((bf16[32,4,4096]{2,1,0:T(4,128)(2,1)}), bf16[32,4,4096]{2,1,0:T(4,128)(2,1)S(1)}, u32[]{:S(2)}, u32[]{:S(2)}) %all-to-all-start.3) | async-done | bytes 1048608 | tf_op jit(solution)/shard_map/all_to_all | solution.py:89
  158.7 0.3 reshape.415
  159.0 0.9 gather_fusion.3
  159.9 0.9 fusion.6
  160.8 0.7 pad_maximum_fusion
  (11 shorter events, 0.1 us)
Async XLA Ops:
  6.0 31.3 %all-to-all-start = ((bf16[32,4,4096]{2,1,0:T(4,128)(2,1)}), bf16[32,4,4096]{2,1,0:T(4,128)(2,1)S(1)}, u32[]{:S(2)}, u32[]{:S(2)}) async-start(bf16[32,4,4096]{2,1,0:T(4,128)(2,1)} %reshape.419), calls=%async_computation | async-start | bytes 2097152 | tf_op jit(solution)/shard_map/all_to_all | solution.py:80
  37.3 29.9 %all-to-all-start.2 = ((bf16[32,4,4096]{2,1,0:T(4,128)(2,1)}), bf16[32,4,4096]{2,1,0:T(4,128)(2,1)}, u32[]{:S(2)}, u32[]{:S(2)}) async-start(bf16[32,4,4096]{2,1,0:T(4,128)(2,1)} %reshape.435), calls=%async_computation.2 | async-start | bytes 2097152 | tf_op jit(solution)/shard_map/all_to_all | solution.py:80
  41.9 25.4 %collective-permute-start = (bf16[32,4,4096]{2,1,0:T(4,128)(2,1)S(1)}, bf16[32,4,4096]{2,1,0:T(4,128)(2,1)S(1)}, u32[]{:S(2)}, u32[]{:S(2)}) collective-permute-start(bf16[32,4,4096]{2,1,0:T(4,128)(2,1)S(1)} %all-to-all-done), channel_id=1, source_target_pairs={{0,1},{1,0},{2,3},{3,2},{4,5},{5,4},{6,7},{7,6},{8,9},{9,8},{10,11... | collective-permute-start | bytes 3145736 | tf_op jit(solution)/shard_map/ppermute | solution.py:12
  67.3 13.8 %collective-permute-start.2 = (bf16[32,4,4096]{2,1,0:T(4,128)(2,1)}, bf16[32,4,4096]{2,1,0:T(4,128)(2,1)}, u32[]{:S(2)}, u32[]{:S(2)}) collective-permute-start(bf16[32,4,4096]{2,1,0:T(4,128)(2,1)} %all-to-all-done.2), channel_id=1, source_target_pairs={{0,1},{1,0},{2,3},{3,2},{4,5},{5,4},{6,7},{7,6},{8,9},{9,8},{10,11... | collective-permute-start | bytes 3145736 | tf_op jit(solution)/shard_map/ppermute | solution.py:12
  67.4 1.0 copy-start.1
  80.7 16.7 %collective-permute-start.1 = (bf16[32,4,4096]{2,1,0:T(4,128)(2,1)}, bf16[32,4,4096]{2,1,0:T(4,128)(2,1)S(1)}, u32[]{:S(2)}, u32[]{:S(2)}) collective-permute-start(bf16[32,4,4096]{2,1,0:T(4,128)(2,1)} %slice.49), channel_id=1, source_target_pairs={{0,1},{1,0},{2,3},{3,2},{4,5},{5,4},{6,7},{7,6},{8,9},{9,8},{10,11... | collective-permute-start | bytes 3145736 | tf_op jit(solution)/shard_map/ppermute | solution.py:12
  97.3 6.3 %collective-permute-start.3 = (bf16[32,4,4096]{2,1,0:T(4,128)(2,1)}, bf16[32,4,4096]{2,1,0:T(4,128)(2,1)}, u32[]{:S(2)}, u32[]{:S(2)}) collective-permute-start(bf16[32,4,4096]{2,1,0:T(4,128)(2,1)} %slice.51), channel_id=1, source_target_pairs={{0,1},{1,0},{2,3},{3,2},{4,5},{5,4},{6,7},{7,6},{8,9},{9,8},{10,11... | collective-permute-start | bytes 3145736 | tf_op jit(solution)/shard_map/ppermute | solution.py:12
  99.0 34.4 %copy-start = (s32[2,8,8]{2,1,0:T(8,128)S(1)}, s32[2,8,8]{2,1,0:T(8,128)}, u32[]{:S(2)}) copy-start(s32[2,8,8]{2,1,0:T(8,128)} %param.8) | copy-start | bytes 1540
  99.0 29.8 %all-to-all-start.1 = ((bf16[32,4,4096]{2,1,0:T(4,128)(2,1)}), bf16[32,4,4096]{2,1,0:T(4,128)(2,1)S(1)}, u32[]{:S(2)}, u32[]{:S(2)}) async-start(bf16[32,4,4096]{2,1,0:T(4,128)(2,1)} %add_convert_fusion.1), calls=%async_computation.1 | async-start | bytes 2097152 | tf_op jit(solution)/shard_map/all_to_all | solution.py:89
  128.9 29.8 %all-to-all-start.3 = ((bf16[32,4,4096]{2,1,0:T(4,128)(2,1)}), bf16[32,4,4096]{2,1,0:T(4,128)(2,1)S(1)}, u32[]{:S(2)}, u32[]{:S(2)}) async-start(bf16[32,4,4096]{2,1,0:T(4,128)(2,1)} %add_convert_fusion), calls=%async_computation.3 | async-start | bytes 2097152 | tf_op jit(solution)/shard_map/all_to_all | solution.py:89
where the time goes:
time: 164 us; the launch traced here: 161 us
  waiting for transfers between devices  91.5 us (56%)
  matrix products  23.7 us (14%)
  starting transfers between devices  20.5 us (12%)
  local copies, waits for them, and re-layouts  16.8 us (10%)
  other arithmetic  8.65 us (5%)
    all_to_all x2, waiting for transfers between devices, shards(): lax.all_to_all(send_rows, 'expert', split_axis=0, concat_axis=0, tiled=True)  46.1 us
    all_to_all x2, waiting for transfers between devices, shards(): lax.all_to_all(summed, 'expert', split_axis=0, concat_axis=0, tiled=True)  45.5 us
    dot_general x2, matrix products, half_expert(): jnp.dot(hidden, down_half, preferred_element_type=jnp.float32)  14.5 us
    all_to_all x2, starting transfers between devices, shards(): lax.all_to_all(send_rows, 'expert', split_axis=0, concat_axis=0, tiled=True)  10.6 us
    dot_general x2, matrix products, half_expert(): up_value = jnp.dot(step_rows, up_half, preferred_element_type=jnp.float32)  9.18 us
    all_to_all x2, starting transfers between devices, shards(): lax.all_to_all(summed, 'expert', split_axis=0, concat_axis=0, tiled=True)  9.06 us
    convert_element_type x2, other arithmetic, shards(): summed = (produced[:, :own_count].astype(jnp.float32) + from_partner.asty...  5.34 us
    gather x4, local copies, waits for them, and re-layouts, shards(): send_rows = padded_rows[owner_slot]  4.86 us
  transfers between devices with their start and end apart: 8, of which 4 were waited for; matrix products, arithmetic and copies ran while one was open for 25% of the time, Pallas kernels for 0%

commit v1 on v0

v1 whole, which is shorter than its diff:
```python
import jax
import jax.numpy as jnp
from jax import lax
from jax.sharding import PartitionSpec as P

route_scale = 2.5


def dense_gates(id_block, code_block, expert_count):
    code_rows = code_block.astype(jnp.float32)
    weights = route_scale * code_rows / jnp.sum(code_rows, axis=-1, keepdims=True)
    hit = id_block[..., None] == jnp.arange(expert_count, dtype=jnp.int32)
    return jnp.sum(jnp.where(hit, weights[..., None], 0.0), axis=-2)


def shards(hidden_rows, expert_ids, gate_codes, gate_weight, up_weight, down_weight):
    peer_count = lax.axis_size("expert")
    expert_count = peer_count // 2
    micro_count, rows_dev, feature_count = hidden_rows.shape
    own_expert = lax.axis_index("expert") // 2
    gates = dense_gates(expert_ids, gate_codes, expert_count)
    all_gates = lax.all_gather(gates.reshape(micro_count * rows_dev, expert_count), "expert")
    all_rows = lax.all_gather(
        hidden_rows.reshape(micro_count * rows_dev, feature_count), "expert", tiled=True
    )
    own_gate = lax.dynamic_index_in_dim(all_gates, own_expert, 2, keepdims=False).reshape(-1, 1)
    gate_value = jnp.dot(all_rows, gate_weight, preferred_element_type=jnp.float32)
    up_value = jnp.dot(all_rows, up_weight, preferred_element_type=jnp.float32)
    hidden = (jax.nn.silu(gate_value) * up_value).astype(jnp.bfloat16)
    produced = jnp.dot(hidden, down_weight, preferred_element_type=jnp.float32)
    weighted = (produced * own_gate).astype(jnp.bfloat16)
    combined = lax.psum_scatter(weighted, "expert", scatter_dimension=0, tiled=True)
    return combined.reshape(micro_count, rows_dev, feature_count)


def solution(mesh):
    return jax.shard_map(
        shards,
        mesh=mesh,
        in_specs=(
            P(None, ("groups", "expert"), None),
            P(None, ("groups", "expert"), None),
            P(None, ("groups", "expert"), None),
            P(None, "expert"),
            P(None, "expert"),
            P("expert", None),
        ),
        out_specs=P(None, ("groups", "expert"), None),
        check_vma=False,
    )
```

time: 164 us -> 241 us (1.47)
  the two profiles are of different devices: /device:TPU:8 before, /device:TPU:0 now
where the time goes in v1:
time: 241 us
  waiting for transfers between devices  164 us (68%)
  blocking collectives  44.3 us (18%)
  matrix products  17.1 us (7%)
  between operations  13.4 us (6%)
    reduce_scatter x1, waiting for transfers between devices, shards(): lax.psum_scatter(weighted, 'expert', scatter_dimension=0, tiled=True)  142 us
    all_gather x1, blocking collectives, shards(): lax.all_gather(gates.reshape(micro_count * rows_dev, expert_count), 'expe...  44.3 us
    all_gather x1, waiting for transfers between devices, shards(): lax.all_gather(hidden_rows.reshape(micro_count * rows_dev, feature_count)...  21.2 us
    dot_general x1, matrix products, shards(): produced = jnp.dot(hidden, down_weight, preferred_element_type=jnp.float32)  11.3 us
    dot_general x1, matrix products, shards(): jnp.dot(all_rows, gate_weight, preferred_element_type=jnp.float32)  5.79 us
  transfers between devices with their start and end apart: 2, of which 2 were waited for; matrix products, arithmetic and copies ran while one was open for 1% of the time, Pallas kernels for 0%

profile of v1, /device:TPU:0, one launch (start us, length us, event | category | flops | bytes accessed | tf_op | source)
XLA Modules:
  0.0 240.6 jit_solution(1681874830663990973)
XLA Ops:
  6.5 0.0 all-gather.2.cloned.1.call-start
  6.5 0.7 all-gather.2.cloned.1.call-update
  7.3 0.0 reduce-scatter.2.cloned.1.call-start
  7.3 0.9 multiply_divide_fusion
  8.2 0.8 select_reduce_fusion
  9.0 44.3 %all_gather.7 = f32[32,16,16]{2,1,0:T(8,128)S(1)} all-gather(f32[1,16,16]{2,1,0:T(8,128)S(1)} %bitcast.9), channel_id=1, replica_groups=mesh['groups'=1,'expert'=32] {'expert'}, dimensions={0}, use_global_device_ids=true | all-gather | bytes 33792 | tf_op jit(solution)/shard_map/all_gather | solution.py:22
  53.3 0.2 dynamic-slice_reduce_fusion
  53.5 0.1 mul.27
  53.6 21.2 %all-gather.2.cloned.1.call-done = bf16[512,4096]{1,0:T(8,128)(2,1)} async-done(((bf16[16,4096]{1,0:T(8,128)(2,1)}), bf16[512,4096]{1,0:T(8,128)(2,1)}) %all-gather.2.cloned.1.call-update) | async-done | bytes 4194320 | tf_op jit(solution)/shard_map/all_gather | solution.py:23
  74.8 5.8 %fusion.8 = f32[512,512]{1,0:T(8,128)S(1)} fusion(bf16[512,4096]{1,0:T(8,128)(2,1)} %all-gather.2.cloned.1.call-done, bf16[4096,512]{1,0:T(8,128)(2,1)} %param.9), kind=kOutput, calls=%fused_computation.14 | convolution fusion | flops 2147483648 | bytes 9437184 | tf_op jit(solution)/shard_map/dot_general | solution.py:27
  80.6 11.3 %multiply_convert_fusion = bf16[512,4096]{1,0:T(8,128)(2,1)} fusion(bf16[512,4096]{1,0:T(8,128)(2,1)} %param.11, f32[512]{0:T(512)S(1)} %mul.27, bf16[512,4096]{1,0:T(8,128)(2,1)} %all-gather.2.cloned.1.call-done, bf16[4096,512]{1,0:T(8,128)(2,1)} %param.10, f32[512,512]{1,0:T(8,128)S(1)} %fusion.8), kind=kOutput, calls=%fused_computation | convolution fusion | flops 4300734464 | bytes 17827840 | tf_op jit(solution)/shard_map/dot_general | solution.py:30
  91.9 0.0 reduce-scatter.2.cloned.1.call-update
  91.9 141.9 %reduce-scatter.2.cloned.1.call-done = bf16[16,4096]{1,0:T(8,128)(2,1)} async-done(((bf16[512,4096]{1,0:T(8,128)(2,1)}), bf16[16,4096]{1,0:T(8,128)(2,1)}) %reduce-scatter.2.cloned.1.call-update) | async-done | bytes 131088 | tf_op jit(solution)/shard_map/reduce_scatter | solution.py:32
Async XLA Ops:
  6.5 68.3 %all-gather.2.cloned.1.call-start = ((), (), s32[]{:S(2)}) async-start(), calls=%async_computation.1 | async-start | bytes 4325376 | tf_op jit(solution)/shard_map/all_gather | solution.py:23
  7.3 226.5 %reduce-scatter.2.cloned.1.call-start = ((), (), s32[]{:S(2)}) async-start(), calls=%async_computation.2 | async-start | bytes 4325376 | tf_op jit(solution)/shard_map/reduce_scatter | solution.py:32
Sparse Core Ops, SparseCore 0:
  10.2 64.5 all-gather.1
  92.0 141.7 reduce-scatter.1

commit v2 on v1

v2 whole, which is shorter than its diff:
```python
import functools

import jax
import jax.numpy as jnp
from jax import lax
from jax.experimental import pallas as pl
from jax.experimental.pallas import tpu as pltpu
from jax.sharding import PartitionSpec as P

route_scale = 2.5
LANES = 128


def place(n):
    me = lax.axis_index("expert")
    core, x, y, z = me % 2, (me // 2) % 2, (me // 4) % 2, me // 8
    to_y, to_x = me + 4 - 8 * y, me + 2 - 4 * x
    return dict(
        me=me, core=core, z=z, lines=n // 8,
        near=to_y * (1 - core) + to_x * core,
        far=to_x * (1 - core) + to_y * core,
        twin=me + 1 - 2 * core,
        i1=y * (1 - core) + x * core,
        i2=x * (1 - core) + y * core,
    )


def greet(at):
    barrier = pltpu.get_barrier_semaphore()
    z, lines = at["z"], at["lines"]

    def signal(device):
        pl.semaphore_signal(
            barrier, inc=1, device_id={"expert": device},
            device_id_type=pl.DeviceIdType.MESH,
        )

    for name in ("near", "far", "twin"):
        signal(at[name])

    @pl.when(z > 0)
    def _():
        signal(at["me"] - 8)

    @pl.when(z < lines - 1)
    def _():
        signal(at["me"] + 8)

    on_line = (z + lines - 1) // lines + (2 * lines - 2 - z) // lines
    pl.semaphore_wait(barrier, 3 + on_line)


def remote(src, dst, send_sem, recv_sem, device):
    return pltpu.make_async_remote_copy(
        src_ref=src, dst_ref=dst, send_sem=send_sem, recv_sem=recv_sem,
        device_id={"expert": device}, device_id_type=pl.DeviceIdType.MESH,
    )


def gather_kernel(n, own_ref, out_ref, send_sem, recv_sem):
    at = place(n)
    me, z, lines = at["me"], at["z"], at["lines"]
    near, far, twin = at["near"], at["far"], at["twin"]
    both = near + far - me
    greet(at)

    def send(kind, source, device, begin, first=False):
        copy = remote(
            own_ref if first else out_ref.at[source], out_ref.at[source],
            send_sem.at[kind, source], recv_sem.at[source], device,
        )
        if begin:
            copy.start()
        else:
            copy.wait_send()

    def arrived(source):
        remote(
            out_ref.at[source], out_ref.at[source],
            send_sem.at[0, source], recv_sem.at[source], twin,
        ).wait_recv()

    def line_sends(source, begin, up, down, first=False):
        if up:
            @pl.when(z < lines - 1)
            def _():
                send(0, source, me + 8, begin, first)
        if down:
            @pl.when(z > 0)
            def _():
                send(1, source, me - 8, begin, first)
        send(2, source, near, begin, first)
        send(3, source, far, begin, first)
        send(4, source, twin, begin, first)

    def line_step(k, begin):
        @pl.when(z >= k)
        def _():
            if begin:
                arrived(me - 8 * k)
            line_sends(me - 8 * k, begin, True, False)

        @pl.when(z + k < lines)
        def _():
            if begin:
                arrived(me + 8 * k)
            line_sends(me + 8 * k, begin, False, True)

    def side_step(base, k, to_far, begin):
        def one(source):
            if begin:
                arrived(source)
            if to_far:
                send(3, source, far, begin)
            send(4, source, twin, begin)

        if k == 0:
            one(base)
            return

        @pl.when(z >= k)
        def _():
            one(base - 8 * k)

        @pl.when(z + k < lines)
        def _():
            one(base + 8 * k)

    line_sends(me, True, True, True, True)
    out_ref[me] = own_ref[...]
    for k in range(1, lines + 3):
        if k < lines:
            line_step(k, True)
        if k - 1 < lines:
            side_step(near, k - 1, True, True)
        if 0 <= k - 2 < lines:
            side_step(far, k - 2, False, True)
        if 0 <= k - 3 < lines:
            side_step(both, k - 3, False, True)
    for chip in range(n // 2):
        arrived(2 * chip + 1 - at["core"])
    line_sends(me, False, True, True, True)
    for k in range(lines):
        if k > 0:
            line_step(k, False)
        side_step(near, k, True, False)
        side_step(far, k, False, False)
        side_step(both, k, False, False)


def scatter_kernel(
    n, part_ref, out_ref, twin_in, far_in, near_in, down_in, up_in, out_far, out_near, out_line,
    twin_send, twin_recv, far_send, far_recv, near_send, near_recv,
    down_send, down_recv, up_send, up_recv,
):
    at = place(n)
    me, z, lines, core = at["me"], at["z"], at["lines"], at["core"]
    near, far, twin, i1, i2 = at["near"], at["far"], at["twin"], at["i1"], at["i2"]
    greet(at)
    order = []
    for step in range((lines + 1) // 2):
        order.append(step)
        if lines - 1 - step != step:
            order.append(lines - 1 - step)

    def chip(line, j1, j2, c):
        m1 = 2 - c
        m2 = 1 + c
        return line * 4 + j1 * m1 + j2 * m2

    def f32(value):
        return value.astype(jnp.float32)

    def to_twin(line, j1, j2):
        slot = chip(line, j1, j2, 1 - core)
        return remote(
            part_ref.at[2 * slot + 1 - core], twin_in.at[slot],
            twin_send.at[slot], twin_recv.at[slot], twin,
        )

    groups = ((1 - i1, 1 - i2), (i1, 1 - i2))
    twin_groups = ((1 - i2, 1 - i1), (i2, 1 - i1), (1 - i2, i1), (i2, i1))
    for j1, j2 in twin_groups:
        for line in order:
            to_twin(line, j1, j2).start()

    def pair(line, j1, j2):
        slot = chip(line, j1, j2, core)
        remote(
            twin_in.at[slot], twin_in.at[slot], twin_send.at[slot], twin_recv.at[slot], twin
        ).wait_recv()
        return f32(part_ref[2 * slot + core]) + f32(twin_in[slot])

    def to_far(line, j1):
        slot = line * 2 + j1
        return remote(
            out_far.at[slot], far_in.at[slot], far_send.at[slot], far_recv.at[slot], far
        )

    def to_near(line):
        return remote(
            out_near.at[line], near_in.at[line], near_send.at[line], near_recv.at[line], near
        )

    def to_down(line):
        return remote(
            out_line.at[line], down_in.at[line], down_send.at[line], down_recv.at[line], me - 8
        )

    def to_up(line):
        return remote(
            out_line.at[line], up_in.at[line], up_send.at[line], up_recv.at[line], me + 8
        )

    for j1, j2 in groups:
        for line in order:
            out_far[line * 2 + j1] = pair(line, j1, j2).astype(jnp.bfloat16)
            to_far(line, j1).start()

    def after_far(line, j1):
        value = pair(line, j1, i2)
        to_far(line, j1).wait_recv()
        return value + f32(far_in[line * 2 + j1])

    for line in order:
        out_near[line] = after_far(line, 1 - i1).astype(jnp.bfloat16)
        to_near(line).start()

    def after_near(line):
        value = after_far(line, i1)
        to_near(line).wait_recv()
        return value + f32(near_in[line])

    for line in order:
        @pl.when(z > line)
        def _():
            value = after_near(line)

            @pl.when(z < lines - 1)
            def _():
                to_down(line).wait_recv()
                out_line[line] = (value + f32(down_in[line])).astype(jnp.bfloat16)

            @pl.when(z == lines - 1)
            def _():
                out_line[line] = value.astype(jnp.bfloat16)

            to_down(line).start()

        @pl.when(z < line)
        def _():
            value = after_near(line)

            @pl.when(z > 0)
            def _():
                to_up(line).wait_recv()
                out_line[line] = (value + f32(up_in[line])).astype(jnp.bfloat16)

            @pl.when(z == 0)
            def _():
                out_line[line] = value.astype(jnp.bfloat16)

            to_up(line).start()

    final = after_near(z)

    @pl.when(z == 0)
    def _():
        to_down(z).wait_recv()
        out_ref[...] = (final + f32(down_in[z])).astype(jnp.bfloat16)

    @pl.when(z == lines - 1)
    def _():
        to_up(z).wait_recv()
        out_ref[...] = (final + f32(up_in[z])).astype(jnp.bfloat16)

    @pl.when((z > 0) & (z < lines - 1))
    def _():
        to_down(z).wait_recv()
        to_up(z).wait_recv()
        out_ref[...] = (final + f32(down_in[z]) + f32(up_in[z])).astype(jnp.bfloat16)

    for line in range(lines):
        for j1 in range(2):
            to_far(line, j1).wait_send()
            for j2 in range(2):
                to_twin(line, j1, j2).wait_send()
        to_near(line).wait_send()

        @pl.when(z > line)
        def _():
            to_down(line).wait_send()

        @pl.when(z < line)
        def _():
            to_up(line).wait_send()


def gather_rows(own, n):
    return pl.pallas_call(
        functools.partial(gather_kernel, n),
        out_shape=jax.ShapeDtypeStruct((n,) + own.shape, own.dtype),
        in_specs=[pl.BlockSpec(memory_space=pltpu.VMEM)],
        out_specs=pl.BlockSpec(memory_space=pltpu.VMEM),
        scratch_shapes=[pltpu.SemaphoreType.DMA((5, n)), pltpu.SemaphoreType.DMA((n,))],
        compiler_params=pltpu.CompilerParams(
            collective_id=0, has_side_effects=True, vmem_limit_bytes=60 * 2**20
        ),
        name="gather_rows",
    )(own)


def scatter_sums(parts, n):
    block = parts.shape[1:]
    lines = n // 8

    def room(count):
        return pltpu.VMEM((count,) + block, jnp.bfloat16)

    counts = [n // 2, n // 2, 2 * lines, 2 * lines] + [lines] * 6
    return pl.pallas_call(
        functools.partial(scatter_kernel, n),
        out_shape=jax.ShapeDtypeStruct(block, jnp.bfloat16),
        in_specs=[pl.BlockSpec(memory_space=pltpu.VMEM)],
        out_specs=pl.BlockSpec(memory_space=pltpu.VMEM),
        scratch_shapes=[
            room(n // 2), room(2 * lines), room(lines), room(lines), room(lines),
            room(2 * lines), room(lines), room(lines),
        ] + [pltpu.SemaphoreType.DMA((count,)) for count in counts],
        compiler_params=pltpu.CompilerParams(
            collective_id=1, has_side_effects=True, vmem_limit_bytes=60 * 2**20
        ),
        name="scatter_sums",
    )(parts)


def dense_gates(id_block, code_block, expert_count):
    code_rows = code_block.astype(jnp.float32)
    weights = route_scale * code_rows / jnp.sum(code_rows, axis=-1, keepdims=True)
    hit = id_block[..., None] == jnp.arange(expert_count, dtype=jnp.int32)
    return jnp.sum(jnp.where(hit, weights[..., None], 0.0), axis=-2)


def shards(hidden_rows, expert_ids, gate_codes, gate_weight, up_weight, down_weight):
    n = lax.axis_size("expert")
    expert_count = n // 2
    micro_count, rows_dev, feature_count = hidden_rows.shape
    block_rows = micro_count * rows_dev
    own_expert = lax.axis_index("expert") // 2
    gates = dense_gates(expert_ids, gate_codes, expert_count).reshape(block_rows, expert_count)
    high = lax.reduce_precision(gates, 8, 7)
    width = -(-2 * expert_count // LANES) * LANES
    tail = jnp.concatenate([high, gates - high], axis=1).astype(jnp.bfloat16)
    tail = jnp.pad(tail, ((0, 0), (0, width - 2 * expert_count)))
    own = jnp.concatenate([hidden_rows.reshape(block_rows, feature_count), tail], axis=1)
    gathered = gather_rows(own, n).reshape(n * block_rows, feature_count + width)
    all_rows = gathered[:, :feature_count]
    tails = gathered[:, feature_count:].astype(jnp.float32)
    lane = jnp.arange(width, dtype=jnp.int32)
    mine = (lane == own_expert) | (lane == own_expert + expert_count)
    own_gate = jnp.sum(jnp.where(mine, tails, 0.0), axis=1, keepdims=True)
    gate_value = jnp.dot(all_rows, gate_weight, preferred_element_type=jnp.float32)
    up_value = jnp.dot(all_rows, up_weight, preferred_element_type=jnp.float32)
    hidden = (jax.nn.silu(gate_value) * up_value).astype(jnp.bfloat16)
    produced = jnp.dot(hidden, down_weight, preferred_element_type=jnp.float32)
    weighted = (produced * own_gate).astype(jnp.bfloat16)
    combined = scatter_sums(weighted.reshape(n, block_rows, feature_count), n)
    return combined.reshape(micro_count, rows_dev, feature_count)


def solution(mesh):
    return jax.shard_map(
        shards,
        mesh=mesh,
        in_specs=(
            P(None, ("groups", "expert"), None),
            P(None, ("groups", "expert"), None),
            P(None, ("groups", "expert"), None),
            P(None, "expert"),
            P(None, "expert"),
            P("expert", None),
        ),
        out_specs=P(None, ("groups", "expert"), None),
        check_vma=False,
    )
```

time: 241 us -> 89.1 us (0.37)
  the two profiles are of different devices: /device:TPU:0 before, /device:TPU:8 now
where the time goes in v2:
time: 89.1 us; the launch traced here: 88.4 us
  Pallas kernels  65.4 us (73%)
  matrix products  17.1 us (19%)
  other arithmetic  4.33 us (5%)
  local copies, waits for them, and re-layouts  1.57 us (2%)
    pallas_call x1, Pallas kernels, scatter_sums(): pl.pallas_call(functools.partial(scatter_kernel, n), out_shape=jax.ShapeD...  38.3 us
    pallas_call x1, Pallas kernels, gather_rows(): pl.pallas_call(functools.partial(gather_kernel, n), out_shape=jax.ShapeDt...  27.1 us
    dot_general x1, matrix products, shards(): produced = jnp.dot(hidden, down_weight, preferred_element_type=jnp.float32)  11.3 us
    dot_general x1, matrix products, shards(): jnp.dot(all_rows, gate_weight, preferred_element_type=jnp.float32)  5.79 us

profile of v2, /device:TPU:8, one launch (start us, length us, event | category | flops | bytes accessed | tf_op | source)
XLA Modules:
  0.0 88.4 jit_solution(11125544669036335461)
XLA Ops:
  0.0 0.9 multiply_divide_fusion
  0.9 0.8 select_reduce_fusion.1
  1.7 0.1 fusion.17
  1.8 1.6 %pad_maximum_fusion.own_ref = bf16[16,4224]{1,0:T(8,128)(2,1)} fusion(bf16[16,128]{1,0:T(8,128)(2,1)S(1)} %fusion.17, bf16[16,4096]{1,0:T(8,128)(2,1)} %bitcast.15), kind=kLoop, calls=%fused_computation.9 | loop fusion | flops 270336 | bytes 270336 | tf_op jit(solution)/shard_map/concatenate | solution.py:355
  3.3 27.1 %gather_rows.1 = bf16[32,16,4224]{2,1,0:T(8,128)(2,1)} custom-call(bf16[16,4224]{1,0:T(8,128)(2,1)} %pad_maximum_fusion.own_ref), custom_call_target="tpu_custom_call" | custom-call | tf_op jit(solution)/shard_map/gather_rows/pallas_call | solution.py:300
  30.5 1.0 %select_reduce_fusion = f32[512]{0:T(512)S(1)} fusion(bf16[512,4224]{1,0:T(8,128)(2,1)} %bitcast.10, pred[128]{0:T(512)(128)(4,1)S(1)} %compare_or_fusion), kind=kLoop, calls=%fused_computation.8 | loop fusion | flops 196096 | bytes 133248 | tf_op jit(solution)/shard_map/reduce_sum | solution.py:361
  31.5 5.8 %fusion.2 = f32[512,512]{1,0:T(8,128)S(1)} fusion(bf16[4096,512]{1,0:T(8,128)(2,1)} %param.9, bf16[512,4224]{1,0:T(8,128)(2,1)} %bitcast.11), kind=kOutput, calls=%fused_computation.3 | convolution fusion | flops 2147483648 | bytes 9437184 | tf_op jit(solution)/shard_map/dot_general | solution.py:362
  37.3 11.3 %multiply_convert_fusion = bf16[512,4096]{1,0:T(8,128)(2,1)} fusion(bf16[512,4096]{1,0:T(8,128)(2,1)} %param.11, f32[512]{0:T(512)S(1)} %select_reduce_fusion, bf16[4096,512]{1,0:T(8,128)(2,1)} %param.10, bf16[512,4224]{1,0:T(8,128)(2,1)} %bitcast.12, f32[512,512]{1,0:T(8,128)S(1)} %fusion.2), kind=kOutput, calls=%fused_computation | convolution fusion | flops 4300734464 | bytes 17827840 | tf_op jit(solution)/shard_map/dot_general | solution.py:365
  48.6 38.3 %scatter_sums.1 = bf16[16,4096]{1,0:T(8,128)(2,1)} custom-call(bf16[32,16,4096]{2,1,0:T(8,128)(2,1)} %bitcast.13), custom_call_target="tpu_custom_call" | custom-call | tf_op jit(solution)/shard_map/scatter_sums/pallas_call | solution.py:321
  86.9 1.6 %copy.8 = bf16[2,8,4096]{2,1,0:T(8,128)(2,1)} copy(bf16[2,8,4096]{2,1,0:T(8,128)(2,1)} %bitcast.14) | data formatting | bytes 262144
  (2 shorter events, 0.0 us)

commit v3 on v2

--- a/solution.py
+++ b/solution.py
@@ -1,4 +1,5 @@
 import functools
+import math
 
 import jax
 import jax.numpy as jnp
@@ -57,7 +58,7 @@
     )
 
 
-def gather_kernel(n, own_ref, out_ref, send_sem, recv_sem):
+def gather_kernel(n, own_ref, out_ref, send_sem, recv_sem, work=None, between=None):
     at = place(n)
     me, z, lines = at["me"], at["z"], at["lines"]
     near, far, twin = at["near"], at["far"], at["twin"]
@@ -128,17 +129,30 @@
 
     line_sends(me, True, True, True, True)
     out_ref[me] = own_ref[...]
-    for k in range(1, lines + 3):
+    def twins_arrived(group):
+        for line in range(lines):
+            arrived(group + 8 * line + 1 - at["core"])
+
+    def work_on(device):
+        group = device - at["core"] - 8 * z
+        twins_arrived(group)
+        if work is not None:
+            work(group)
+
+    for k in range(1, lines + 1):
         if k < lines:
             line_step(k, True)
-        if k - 1 < lines:
-            side_step(near, k - 1, True, True)
-        if 0 <= k - 2 < lines:
-            side_step(far, k - 2, False, True)
-        if 0 <= k - 3 < lines:
-            side_step(both, k - 3, False, True)
-    for chip in range(n // 2):
-        arrived(2 * chip + 1 - at["core"])
+        side_step(near, k - 1, True, True)
+    work_on(me)
+    for k in range(lines):
+        side_step(far, k, False, True)
+    work_on(near)
+    for k in range(lines):
+        side_step(both, k, False, True)
+    work_on(far)
+    if between is not None:
+        between()
+    work_on(both)
     line_sends(me, False, True, True, True)
     for k in range(lines):
         if k > 0:
@@ -149,6 +163,20 @@
 
 
 def scatter_kernel(
+    n, part_ref, *refs
+):
+    at = place(n)
+    greet(at)
+    start_twins, far_sends, finish = scatter_pieces(n, part_ref, *refs)
+    near, far, me = at["near"], at["far"], at["me"]
+    for device in (near + far - me, far, near, me):
+        start_twins(device - at["core"] - 8 * at["z"])
+    far_sends(False)
+    far_sends(True)
+    finish()
+
+
+def scatter_pieces(
     n, part_ref, out_ref, twin_in, far_in, near_in, down_in, up_in, out_far, out_near, out_line,
     twin_send, twin_recv, far_send, far_recv, near_send, near_recv,
     down_send, down_recv, up_send, up_recv,
@@ -156,7 +184,6 @@
     at = place(n)
     me, z, lines, core = at["me"], at["z"], at["lines"], at["core"]
     near, far, twin, i1, i2 = at["near"], at["far"], at["twin"], at["i1"], at["i2"]
-    greet(at)
     order = []
     for step in range((lines + 1) // 2):
         order.append(step)
@@ -171,18 +198,15 @@
     def f32(value):
         return value.astype(jnp.float32)
 
-    def to_twin(line, j1, j2):
-        slot = chip(line, j1, j2, 1 - core)
+    def to_twin(slot):
         return remote(
             part_ref.at[2 * slot + 1 - core], twin_in.at[slot],
             twin_send.at[slot], twin_recv.at[slot], twin,
         )
 
-    groups = ((1 - i1, 1 - i2), (i1, 1 - i2))
-    twin_groups = ((1 - i2, 1 - i1), (i2, 1 - i1), (1 - i2, i1), (i2, i1))
-    for j1, j2 in twin_groups:
+    def start_twins(group):
         for line in order:
-            to_twin(line, j1, j2).start()
+            to_twin(group // 2 + 4 * line).start()
 
     def pair(line, j1, j2):
         slot = chip(line, j1, j2, core)
@@ -212,9 +236,10 @@
             out_line.at[line], up_in.at[line], up_send.at[line], up_recv.at[line], me + 8
         )
 
-    for j1, j2 in groups:
+    def far_sends(both):
+        j1 = 1 - i1 if both else i1
         for line in order:
-            out_far[line * 2 + j1] = pair(line, j1, j2).astype(jnp.bfloat16)
+            out_far[line * 2 + j1] = pair(line, j1, 1 - i2).astype(jnp.bfloat16)
             to_far(line, j1).start()
 
     def after_far(line, j1):
@@ -222,78 +247,191 @@
         to_far(line, j1).wait_recv()
         return value + f32(far_in[line * 2 + j1])
 
-    for line in order:
-        out_near[line] = after_far(line, 1 - i1).astype(jnp.bfloat16)
-        to_near(line).start()
-
-    def after_near(line):
-        value = after_far(line, i1)
-        to_near(line).wait_recv()
-        return value + f32(near_in[line])
-
-    for line in order:
-        @pl.when(z > line)
-        def _():
-            value = after_near(line)
-
-            @pl.when(z < lines - 1)
+    def finish():
+        for line in order:
+            out_near[line] = after_far(line, 1 - i1).astype(jnp.bfloat16)
+            to_near(line).start()
+
+        def after_near(line):
+            value = after_far(line, i1)
+            to_near(line).wait_recv()
+            return value + f32(near_in[line])
+
+        for line in order:
+            @pl.when(z > line)
             def _():
-                to_down(line).wait_recv()
-                out_line[line] = (value + f32(down_in[line])).astype(jnp.bfloat16)
-
-            @pl.when(z == lines - 1)
+                value = after_near(line)
+
+                @pl.when(z < lines - 1)
+                def _():
+                    to_down(line).wait_recv()
+                    out_line[line] = (value + f32(down_in[line])).astype(jnp.bfloat16)
+
+                @pl.when(z == lines - 1)
+                def _():
+                    out_line[line] = value.astype(jnp.bfloat16)
+
+                to_down(line).start()
+
+            @pl.when(z < line)
             def _():
-                out_line[line] = value.astype(jnp.bfloat16)
-
-            to_down(line).start()
-
-        @pl.when(z < line)
-        def _():
-            value = after_near(line)
-
-            @pl.when(z > 0)
+                value = after_near(line)
+
+                @pl.when(z > 0)
+                def _():
+                    to_up(line).wait_recv()
+                    out_line[line] = (value + f32(up_in[line])).astype(jnp.bfloat16)
+
+                @pl.when(z == 0)
+                def _():
+                    out_line[line] = value.astype(jnp.bfloat16)
+
+                to_up(line).start()
+
+        final = after_near(z)
+
+        @pl.when(z == 0)
+        def _():
+            to_down(z).wait_recv()
+            out_ref[...] = (final + f32(down_in[z])).astype(jnp.bfloat16)
+
+        @pl.when(z == lines - 1)
+        def _():
+            to_up(z).wait_recv()
+            out_ref[...] = (final + f32(up_in[z])).astype(jnp.bfloat16)
+
+        @pl.when((z > 0) & (z < lines - 1))
+        def _():
+            to_down(z).wait_recv()
+            to_up(z).wait_recv()
+            out_ref[...] = (final + f32(down_in[z]) + f32(up_in[z])).astype(jnp.bfloat16)
+
+        for line in range(lines):
+            for j1 in range(2):
+                to_far(line, j1).wait_send()
+                for j2 in range(2):
+                    to_twin(4 * line + 2 * j1 + j2).wait_send()
+            to_near(line).wait_send()
+
+            @pl.when(z > line)
             def _():
-                to_up(line).wait_recv()
-                out_line[line] = (value + f32(up_in[line])).astype(jnp.bfloat16)
-
-            @pl.when(z == 0)
+                to_down(line).wait_send()
+
+            @pl.when(z < line)
             def _():
-                out_line[line] = value.astype(jnp.bfloat16)
-
-            to_up(line).start()
-
-    final = after_near(z)
-
-    @pl.when(z == 0)
-    def _():
-        to_down(z).wait_recv()
-        out_ref[...] = (final + f32(down_in[z])).astype(jnp.bfloat16)
-
-    @pl.when(z == lines - 1)
-    def _():
-        to_up(z).wait_recv()
-        out_ref[...] = (final + f32(up_in[z])).astype(jnp.bfloat16)
-
-    @pl.when((z > 0) & (z < lines - 1))
-    def _():
-        to_down(z).wait_recv()
-        to_up(z).wait_recv()
-        out_ref[...] = (final + f32(down_in[z]) + f32(up_in[z])).astype(jnp.bfloat16)
-
-    for line in range(lines):
-        for j1 in range(2):
-            to_far(line, j1).wait_send()
-            for j2 in range(2):
-                to_twin(line, j1, j2).wait_send()
-        to_near(line).wait_send()
-
-        @pl.when(z > line)
-        def _():
-            to_down(line).wait_send()
-
-        @pl.when(z < line)
-        def _():
-            to_up(line).wait_send()
+                to_up(line).wait_send()
+
+    return start_twins, far_sends, finish
+
+
+def fused_kernel(
+    n, own_ref, gate_hbm, up_hbm, down_hbm, out_ref,
+    all_ref, part_ref, gate_ref, up_ref, down_ref, left_ref, act_ref, scale_ref,
+    load_sem, send_sem, recv_sem, *refs
+):
+    at = place(n)
+    lines = n // 8
+    rows, features = part_ref.shape[1:]
+    hidden = act_ref.shape[1]
+    loads = [
+        pltpu.make_async_copy(source, target, load_sem.at[i])
+        for i, (source, target) in enumerate(
+            ((gate_hbm, gate_ref), (up_hbm, up_ref), (down_hbm, down_ref))
+        )
+    ]
+    for load in loads:
+        load.start()
+    start_twins, far_sends, finish = scatter_pieces(n, part_ref, out_ref, *refs)
+    loaded = []
+
+    def work(group):
+        if not loaded:
+            for load in loads:
+                load.wait()
+            loaded.append(True)
+        width = all_ref.shape[2] - features
+        lane = lax.broadcasted_iota(jnp.int32, (rows, width), 1)
+        own_expert = at["me"] // 2
+        mine = (lane == own_expert) | (lane == own_expert + n // 2)
+        for line in range(lines):
+            for core in range(2):
+                index = group + 8 * line + core
+                base = (2 * line + core) * rows
+                left_ref[base:base + rows, :] = all_ref[index, :, :features]
+                tail = all_ref[index, :, features:].astype(jnp.float32)
+                scale = jnp.sum(jnp.where(mine, tail, 0.0), axis=1, keepdims=True)
+                scale_ref[base:base + rows, :] = jnp.broadcast_to(scale, (rows, LANES))
+        step = min(hidden, 2 * LANES)
+
+        @pl.loop(0, hidden // step)
+        def _(tile):
+            columns = pl.ds(pl.multiple_of(tile * step, step), step)
+            gate = jnp.dot(
+                left_ref[...], gate_ref[:, columns], preferred_element_type=jnp.float32
+            )
+            up = jnp.dot(left_ref[...], up_ref[:, columns], preferred_element_type=jnp.float32)
+            act_ref[:, columns] = (gate / (1.0 + jnp.exp(-gate)) * up).astype(jnp.bfloat16)
+
+        wide = min(features, 4 * LANES)
+
+        @pl.loop(0, features // wide)
+        def _(tile):
+            columns = pl.ds(pl.multiple_of(tile * wide, wide), wide)
+            part = jnp.dot(
+                act_ref[...], down_ref[:, columns], preferred_element_type=jnp.float32
+            )
+            part = (part * scale_ref[:, :1]).astype(jnp.bfloat16)
+            for line in range(lines):
+                for core in range(2):
+                    base = (2 * line + core) * rows
+                    part_ref[group + 8 * line + core, :, columns] = part[base:base + rows, :]
+
+        start_twins(group)
+
+    gather_kernel(
+        n, own_ref, all_ref, send_sem, recv_sem, work, lambda: far_sends(False)
+    )
+    far_sends(True)
+    finish()
+
+
+def fused(own, gate_weight, up_weight, down_weight, n):
+    rows = own.shape[0]
+    hidden, features = down_weight.shape
+    lines = n // 8
+    block = (rows, features)
+
+    def room(*shape):
+        return pltpu.VMEM(shape, jnp.bfloat16)
+
+    arrays = [
+        (n,) + own.shape, (n,) + block, gate_weight.shape, up_weight.shape, down_weight.shape,
+        (lines * 2 * rows, features), (lines * 2 * rows, hidden),
+    ]
+    slots = [
+        (count,) + block
+        for count in (n // 2, 2 * lines, lines, lines, lines, 2 * lines, lines, lines)
+    ]
+    counts = [n // 2, n // 2, 2 * lines, 2 * lines] + [lines] * 6
+    if sum(2 * math.prod(shape) for shape in arrays + slots) > 52 * 2**20:
+        return None
+    anywhere = pl.BlockSpec(memory_space=pl.ANY)
+    return pl.pallas_call(
+        functools.partial(fused_kernel, n),
+        out_shape=jax.ShapeDtypeStruct(block, jnp.bfloat16),
+        in_specs=[pl.BlockSpec(memory_space=pltpu.VMEM), anywhere, anywhere, anywhere],
+        out_specs=pl.BlockSpec(memory_space=pltpu.VMEM),
+        scratch_shapes=[room(*shape) for shape in arrays] + [
+            pltpu.VMEM((lines * 2 * rows, LANES), jnp.float32),
+            pltpu.SemaphoreType.DMA((3,)),
+            pltpu.SemaphoreType.DMA((5, n)), pltpu.SemaphoreType.DMA((n,)),
+        ] + [room(*shape) for shape in slots]
+        + [pltpu.SemaphoreType.DMA((count,)) for count in counts],
+        compiler_params=pltpu.CompilerParams(
+            collective_id=2, has_side_effects=True, vmem_limit_bytes=60 * 2**20
+        ),
+        name="fused",
+    )(own, gate_weight, up_weight, down_weight)
 
 
 def gather_rows(own, n):
@@ -353,6 +491,9 @@
     tail = jnp.concatenate([high, gates - high], axis=1).astype(jnp.bfloat16)
     tail = jnp.pad(tail, ((0, 0), (0, width - 2 * expert_count)))
     own = jnp.concatenate([hidden_rows.reshape(block_rows, feature_count), tail], axis=1)
+    combined = fused(own, gate_weight, up_weight, down_weight, n)
+    if combined is not None:
+        return combined.reshape(micro_count, rows_dev, feature_count)
     gathered = gather_rows(own, n).reshape(n * block_rows, feature_count + width)
     all_rows = gathered[:, :feature_count]
     tails = gathered[:, feature_count:].astype(jnp.float32)

time: 89.1 us -> 75 us (0.84)
  matrix products: 17.1 us -> 0 us
  Pallas kernels: 65.4 us -> 69.1 us
  other arithmetic: 4.33 us -> 3.3 us
    dot_general x2 -> x0, matrix products: 17.1 us -> none  [the longest x1 11.3 us: shards(): produced = jnp.dot(hidden, down_weight, preferred_element_type=jnp.float32)]
    pallas_call x2 -> x1, Pallas kernels: 65.4 us -> 69.1 us  [fused(): pl.pallas_call(functools.partial(fused_kernel, n), out_shape=jax.ShapeDty...]
    reduce_sum x1 -> x0, other arithmetic: 1.02 us -> none  [shards(): own_gate = jnp.sum(jnp.where(mine, tails, 0.0), axis=1, keepdims=True)]
where the time goes in v3:
time: 75 us; the launch traced here: 74 us
  Pallas kernels  69.1 us (92%)
  other arithmetic  3.3 us (4%)
  local copies, waits for them, and re-layouts  1.57 us (2%)
    pallas_call x1, Pallas kernels, fused(): pl.pallas_call(functools.partial(fused_kernel, n), out_shape=jax.ShapeDty...  69.1 us
    unnamed x1, local copies, waits for them, and re-layouts  1.57 us
    concatenate x1, other arithmetic, shards(): jnp.concatenate([hidden_rows.reshape(block_rows, feature_count), tail], a...  1.56 us

profile of v3, /device:TPU:8, one launch (start us, length us, event | category | flops | bytes accessed | tf_op | source)
XLA Modules:
  0.0 74.0 jit_solution(1585501102217804198)
XLA Ops:
  0.0 0.9 %multiply_divide_fusion = f32[2,8,8]{2,1,0:T(8,128)S(1)} fusion(s32[2,8,8]{2,1,0:T(8,128)} %param.8), kind=kOutput, calls=%fused_computation.9 | output fusion | flops 535 | bytes 1024 | tf_op jit(solution)/shard_map/div | solution.py:477
  0.9 0.8 %select_reduce_fusion = f32[2,8,16]{2,1,0:T(8,128)S(1)} fusion(f32[2,8,8]{2,1,0:T(8,128)S(1)} %multiply_divide_fusion, s32[2,8,8]{2,1,0:T(8,128)} %param.7), kind=kLoop, calls=%fused_computation.1 | loop fusion | flops 5888 | bytes 2048 | tf_op jit(solution)/shard_map/reduce_sum | solution.py:479
  1.7 0.1 fusion.4
  1.8 1.6 %pad_maximum_fusion.own_ref = bf16[16,4224]{1,0:T(8,128)(2,1)} fusion(bf16[16,128]{1,0:T(8,128)(2,1)S(1)} %fusion.4, bf16[16,4096]{1,0:T(8,128)(2,1)} %bitcast.6), kind=kLoop, calls=%fused_computation | loop fusion | flops 270336 | bytes 270336 | tf_op jit(solution)/shard_map/concatenate | solution.py:493
  3.3 69.1 %fused.1 = bf16[16,4096]{1,0:T(8,128)(2,1)} custom-call(bf16[16,4224]{1,0:T(8,128)(2,1)} %pad_maximum_fusion.own_ref, bf16[4096,512]{1,0:T(8,128)(2,1)} %gate_hbm.1, bf16[4096,512]{1,0:T(8,128)(2,1)} %up_hbm.1, bf16[512,4096]{1,0:T(8,128)(2,1)} %down_hbm.1), custom_call_target="tpu_custom_call" | custom-call | tf_op jit(solution)/shard_map/fused/pallas_call | solution.py:419
  72.4 1.6 %copy.8 = bf16[2,8,4096]{2,1,0:T(8,128)(2,1)} copy(bf16[2,8,4096]{2,1,0:T(8,128)(2,1)} %bitcast.5) | data formatting | bytes 262144
  (1 shorter events, 0.0 us)

commit v4 on v3

--- a/solution.py
+++ b/solution.py
@@ -10,6 +10,12 @@
 
 route_scale = 2.5
 LANES = 128
+PIECES = 2
+
+
+def span(piece, size):
+    step = size // PIECES // LANES * LANES
+    return slice(piece * step, size if piece == PIECES - 1 else (piece + 1) * step)
 
 
 def place(n):
@@ -65,55 +71,63 @@
     both = near + far - me
     greet(at)
 
-    def send(kind, source, device, begin, first=False):
+    def send(kind, source, piece, device, begin, first=False):
+        columns = span(piece, own_ref.shape[1])
+        here = out_ref.at[source, :, columns]
         copy = remote(
-            own_ref if first else out_ref.at[source], out_ref.at[source],
-            send_sem.at[kind, source], recv_sem.at[source], device,
+            own_ref.at[:, columns] if first else here, here,
+            send_sem.at[kind, source * PIECES + piece],
+            recv_sem.at[source * PIECES + piece], device,
         )
         if begin:
             copy.start()
         else:
             copy.wait_send()
 
+    def arrived_piece(source, piece):
+        here = out_ref.at[source, :, span(piece, own_ref.shape[1])]
+        remote(
+            here, here, send_sem.at[0, source * PIECES + piece],
+            recv_sem.at[source * PIECES + piece], twin,
+        ).wait_recv()
+
     def arrived(source):
-        remote(
-            out_ref.at[source], out_ref.at[source],
-            send_sem.at[0, source], recv_sem.at[source], twin,
-        ).wait_recv()
+        for piece in range(PIECES):
+            arrived_piece(source, piece)
 
     def line_sends(source, begin, up, down, first=False):
-        if up:
-            @pl.when(z < lines - 1)
-            def _():
-                send(0, source, me + 8, begin, first)
-        if down:
-            @pl.when(z > 0)
-            def _():
-                send(1, source, me - 8, begin, first)
-        send(2, source, near, begin, first)
-        send(3, source, far, begin, first)
-        send(4, source, twin, begin, first)
+        for piece in range(PIECES):
+            if begin and not first:
+                arrived_piece(source, piece)
+            if up:
+                @pl.when(z < lines - 1)
+                def _():
+                    send(0, source, piece, me + 8, begin, first)
+            if down:
+                @pl.when(z > 0)
+                def _():
+                    send(1, source, piece, me - 8, begin, first)
+            send(2, source, piece, near, begin, first)
+            send(3, source, piece, far, begin, first)
+            send(4, source, piece, twin, begin, first)
 
     def line_step(k, begin):
         @pl.when(z >= k)
         def _():
-            if begin:
-                arrived(me - 8 * k)
             line_sends(me - 8 * k, begin, True, False)
 
         @pl.when(z + k < lines)
         def _():
-            if begin:
-                arrived(me + 8 * k)
             line_sends(me + 8 * k, begin, False, True)
 
     def side_step(base, k, to_far, begin):
         def one(source):
-            if begin:
-                arrived(source)
-            if to_far:
-                send(3, source, far, begin)
-            send(4, source, twin, begin)
+            for piece in range(PIECES):
+                if begin:
+                    arrived_piece(source, piece)
+                if to_far:
+                    send(3, source, piece, far, begin)
+                send(4, source, piece, twin, begin)
 
         if k == 0:
             one(base)
@@ -133,23 +147,22 @@
         for line in range(lines):
             arrived(group + 8 * line + 1 - at["core"])
 
-    def work_on(device):
-        group = device - at["core"] - 8 * z
-        twins_arrived(group)
+    def work_on(*devices):
+        groups = [device - at["core"] - 8 * z for device in devices]
+        for group in groups:
+            twins_arrived(group)
         if work is not None:
-            work(group)
+            work(groups)
 
     for k in range(1, lines + 1):
         if k < lines:
             line_step(k, True)
         side_step(near, k - 1, True, True)
-    work_on(me)
     for k in range(lines):
         side_step(far, k, False, True)
-    work_on(near)
+    work_on(me, near, far)
     for k in range(lines):
         side_step(both, k, False, True)
-    work_on(far)
     if between is not None:
         between()
     work_on(both)
@@ -198,128 +211,137 @@
     def f32(value):
         return value.astype(jnp.float32)
 
-    def to_twin(slot):
+    def moved(source, target, sems, slot, piece, device):
+        columns = span(piece, part_ref.shape[2])
+        send_sem, recv_sem = sems
+        at_sem = slot * PIECES + piece
         return remote(
-            part_ref.at[2 * slot + 1 - core], twin_in.at[slot],
-            twin_send.at[slot], twin_recv.at[slot], twin,
+            source.at[:, columns], target.at[slot, :, columns],
+            send_sem.at[at_sem], recv_sem.at[at_sem], device,
         )
+
+    pieces = range(PIECES)
+
+    def to_twin(slot, piece):
+        source = part_ref.at[2 * slot + 1 - core]
+        return moved(source, twin_in, (twin_send, twin_recv), slot, piece, twin)
 
     def start_twins(group):
         for line in order:
-            to_twin(group // 2 + 4 * line).start()
-
-    def pair(line, j1, j2):
+            for piece in pieces:
+                to_twin(group // 2 + 4 * line, piece).start()
+
+    def pair(line, j1, j2, piece):
+        columns = span(piece, part_ref.shape[2])
         slot = chip(line, j1, j2, core)
-        remote(
-            twin_in.at[slot], twin_in.at[slot], twin_send.at[slot], twin_recv.at[slot], twin
+        moved(
+            twin_in.at[slot], twin_in, (twin_send, twin_recv), slot, piece, twin
         ).wait_recv()
-        return f32(part_ref[2 * slot + core]) + f32(twin_in[slot])
-
-    def to_far(line, j1):
+        return f32(part_ref[2 * slot + core, :, columns]) + f32(twin_in[slot, :, columns])
+
+    def to_far(line, j1, piece):
         slot = line * 2 + j1
-        return remote(
-            out_far.at[slot], far_in.at[slot], far_send.at[slot], far_recv.at[slot], far
-        )
-
-    def to_near(line):
-        return remote(
-            out_near.at[line], near_in.at[line], near_send.at[line], near_recv.at[line], near
-        )
-
-    def to_down(line):
-        return remote(
-            out_line.at[line], down_in.at[line], down_send.at[line], down_recv.at[line], me - 8
-        )
-
-    def to_up(line):
-        return remote(
-            out_line.at[line], up_in.at[line], up_send.at[line], up_recv.at[line], me + 8
-        )
+        return moved(out_far.at[slot], far_in, (far_send, far_recv), slot, piece, far)
+
+    def to_near(line, piece):
+        return moved(out_near.at[line], near_in, (near_send, near_recv), line, piece, near)
+
+    def to_down(line, piece):
+        return moved(out_line.at[line], down_in, (down_send, down_recv), line, piece, me - 8)
+
+    def to_up(line, piece):
+        return moved(out_line.at[line], up_in, (up_send, up_recv), line, piece, me + 8)
 
     def far_sends(both):
         j1 = 1 - i1 if both else i1
         for line in order:
-            out_far[line * 2 + j1] = pair(line, j1, 1 - i2).astype(jnp.bfloat16)
-            to_far(line, j1).start()
-
-    def after_far(line, j1):
-        value = pair(line, j1, i2)
-        to_far(line, j1).wait_recv()
-        return value + f32(far_in[line * 2 + j1])
+            for piece in pieces:
+                columns = span(piece, part_ref.shape[2])
+                value = pair(line, j1, 1 - i2, piece)
+                out_far[line * 2 + j1, :, columns] = value.astype(jnp.bfloat16)
+                to_far(line, j1, piece).start()
+
+    def after_far(line, j1, piece):
+        value = pair(line, j1, i2, piece)
+        to_far(line, j1, piece).wait_recv()
+        return value + f32(far_in[line * 2 + j1, :, span(piece, part_ref.shape[2])])
+
+    def after_near(line, piece):
+        value = after_far(line, i1, piece)
+        to_near(line, piece).wait_recv()
+        return value + f32(near_in[line, :, span(piece, part_ref.shape[2])])
+
+    def line_sends(line, piece, begin):
+        columns = span(piece, part_ref.shape[2])
+
+        def one(copy, edge, landed):
+            value = after_near(line, piece)
+
+            @pl.when(edge)
+            def _():
+                out_line[line, :, columns] = value.astype(jnp.bfloat16)
+
+            @pl.when(jnp.logical_not(edge))
+            def _():
+                copy.wait_recv()
+                total = value + f32(landed[line, :, columns])
+                out_line[line, :, columns] = total.astype(jnp.bfloat16)
+
+            copy.start()
+
+        @pl.when(z > line)
+        def _():
+            if begin:
+                one(to_down(line, piece), z == lines - 1, down_in)
+            else:
+                to_down(line, piece).wait_send()
+
+        @pl.when(z < line)
+        def _():
+            if begin:
+                one(to_up(line, piece), z == 0, up_in)
+            else:
+                to_up(line, piece).wait_send()
 
     def finish():
         for line in order:
-            out_near[line] = after_far(line, 1 - i1).astype(jnp.bfloat16)
-            to_near(line).start()
-
-        def after_near(line):
-            value = after_far(line, i1)
-            to_near(line).wait_recv()
-            return value + f32(near_in[line])
-
+            for piece in pieces:
+                columns = span(piece, part_ref.shape[2])
+                value = after_far(line, 1 - i1, piece)
+                out_near[line, :, columns] = value.astype(jnp.bfloat16)
+                to_near(line, piece).start()
         for line in order:
-            @pl.when(z > line)
+            for piece in pieces:
+                line_sends(line, piece, True)
+        for piece in pieces:
+            columns = span(piece, part_ref.shape[2])
+            final = after_near(z, piece)
+
+            @pl.when(z == 0)
             def _():
-                value = after_near(line)
-
-                @pl.when(z < lines - 1)
-                def _():
-                    to_down(line).wait_recv()
-                    out_line[line] = (value + f32(down_in[line])).astype(jnp.bfloat16)
-
-                @pl.when(z == lines - 1)
-                def _():
-                    out_line[line] = value.astype(jnp.bfloat16)
-
-                to_down(line).start()
-
-            @pl.when(z < line)
+                to_down(z, piece).wait_recv()
+                out_ref[:, columns] = (final + f32(down_in[z, :, columns])).astype(jnp.bfloat16)
+
+            @pl.when(z == lines - 1)
             def _():
-                value = after_near(line)
-
-                @pl.when(z > 0)
-                def _():
-                    to_up(line).wait_recv()
-                    out_line[line] = (value + f32(up_in[line])).astype(jnp.bfloat16)
-
-                @pl.when(z == 0)
-                def _():
-                    out_line[line] = value.astype(jnp.bfloat16)
-
-                to_up(line).start()
-
-        final = after_near(z)
-
-        @pl.when(z == 0)
-        def _():
-            to_down(z).wait_recv()
-            out_ref[...] = (final + f32(down_in[z])).astype(jnp.bfloat16)
-
-        @pl.when(z == lines - 1)
-        def _():
-            to_up(z).wait_recv()
-            out_ref[...] = (final + f32(up_in[z])).astype(jnp.bfloat16)
-
-        @pl.when((z > 0) & (z < lines - 1))
-        def _():
-            to_down(z).wait_recv()
-            to_up(z).wait_recv()
-            out_ref[...] = (final + f32(down_in[z]) + f32(up_in[z])).astype(jnp.bfloat16)
+                to_up(z, piece).wait_recv()
+                out_ref[:, columns] = (final + f32(up_in[z, :, columns])).astype(jnp.bfloat16)
+
+            @pl.when((z > 0) & (z < lines - 1))
+            def _():
+                to_down(z, piece).wait_recv()
+                to_up(z, piece).wait_recv()
+                total = final + f32(down_in[z, :, columns]) + f32(up_in[z, :, columns])
+                out_ref[:, columns] = total.astype(jnp.bfloat16)
 
         for line in range(lines):
-            for j1 in range(2):
-                to_far(line, j1).wait_send()
-                for j2 in range(2):
-                    to_twin(4 * line + 2 * j1 + j2).wait_send()
-            to_near(line).wait_send()
-
-            @pl.when(z > line)
-            def _():
-                to_down(line).wait_send()
-
-            @pl.when(z < line)
-            def _():
-                to_up(line).wait_send()
+            for piece in pieces:
+                for j1 in range(2):
+                    to_far(line, j1, piece).wait_send()
+                    for j2 in range(2):
+                        to_twin(4 * line + 2 * j1 + j2, piece).wait_send()
+                to_near(line, piece).wait_send()
+                line_sends(line, piece, False)
 
     return start_twins, far_sends, finish
 
@@ -344,7 +366,7 @@
     start_twins, far_sends, finish = scatter_pieces(n, part_ref, out_ref, *refs)
     loaded = []
 
-    def work(group):
+    def work(groups):
         if not loaded:
             for load in loads:
                 load.wait()
@@ -353,24 +375,28 @@
         lane = lax.broadcasted_iota(jnp.int32, (rows, width), 1)
         own_expert = at["me"] // 2
         mine = (lane == own_expert) | (lane == own_expert + n // 2)
-        for line in range(lines):
-            for core in range(2):
-                index = group + 8 * line + core
-                base = (2 * line + core) * rows
-                left_ref[base:base + rows, :] = all_ref[index, :, :features]
-                tail = all_ref[index, :, features:].astype(jnp.float32)
-                scale = jnp.sum(jnp.where(mine, tail, 0.0), axis=1, keepdims=True)
-                scale_ref[base:base + rows, :] = jnp.broadcast_to(scale, (rows, LANES))
+        places = [
+            (group + 8 * line + core, ((order * lines + line) * 2 + core) * rows)
+            for order, group in enumerate(groups) for line in range(lines) for core in range(2)
+        ]
+        total = len(places) * rows
+        for index, base in places:
+            left_ref[base:base + rows, :] = all_ref[index, :, :features]
+            tail = all_ref[index, :, features:].astype(jnp.float32)
+            scale = jnp.sum(jnp.where(mine, tail, 0.0), axis=1, keepdims=True)
+            scale_ref[base:base + rows, :] = jnp.broadcast_to(scale, (rows, LANES))
         step = min(hidden, 2 * LANES)
 
         @pl.loop(0, hidden // step)
         def _(tile):
             columns = pl.ds(pl.multiple_of(tile * step, step), step)
             gate = jnp.dot(
-                left_ref[...], gate_ref[:, columns], preferred_element_type=jnp.float32
+                left_ref[:total, :], gate_ref[:, columns], preferred_element_type=jnp.float32
             )
-            up = jnp.dot(left_ref[...], up_ref[:, columns], preferred_element_type=jnp.float32)
-            act_ref[:, columns] = (gate / (1.0 + jnp.exp(-gate)) * up).astype(jnp.bfloat16)
+            up = jnp.dot(
+                left_ref[:total, :], up_ref[:, columns], preferred_element_type=jnp.float32
+            )
+            act_ref[:total, columns] = (gate / (1.0 + jnp.exp(-gate)) * up).astype(jnp.bfloat16)
 
         wide = min(features, 4 * LANES)
 
@@ -378,15 +404,14 @@
         def _(tile):
             columns = pl.ds(pl.multiple_of(tile * wide, wide), wide)
             part = jnp.dot(
-                act_ref[...], down_ref[:, columns], preferred_element_type=jnp.float32
+                act_ref[:total, :], down_ref[:, columns], preferred_element_type=jnp.float32
             )
-            part = (part * scale_ref[:, :1]).astype(jnp.bfloat16)
-            for line in range(lines):
-                for core in range(2):
-                    base = (2 * line + core) * rows
-                    part_ref[group + 8 * line + core, :, columns] = part[base:base + rows, :]
-
-        start_twins(group)
+            part = (part * scale_ref[:total, :1]).astype(jnp.bfloat16)
+            for index, base in places:
+                part_ref[index, :, columns] = part[base:base + rows, :]
+
+        for group in groups:
+            start_twins(group)
 
     gather_kernel(
         n, own_ref, all_ref, send_sem, recv_sem, work, lambda: far_sends(False)
@@ -406,7 +431,7 @@
 
     arrays = [
         (n,) + own.shape, (n,) + block, gate_weight.shape, up_weight.shape, down_weight.shape,
-        (lines * 2 * rows, features), (lines * 2 * rows, hidden),
+        (lines * 6 * rows, features), (lines * 6 * rows, hidden),
     ]
     slots = [
         (count,) + block
@@ -422,11 +447,11 @@
         in_specs=[pl.BlockSpec(memory_space=pltpu.VMEM), anywhere, anywhere, anywhere],
         out_specs=pl.BlockSpec(memory_space=pltpu.VMEM),
         scratch_shapes=[room(*shape) for shape in arrays] + [
-            pltpu.VMEM((lines * 2 * rows, LANES), jnp.float32),
+            pltpu.VMEM((lines * 6 * rows, LANES), jnp.float32),
             pltpu.SemaphoreType.DMA((3,)),
-            pltpu.SemaphoreType.DMA((5, n)), pltpu.SemaphoreType.DMA((n,)),
+            pltpu.SemaphoreType.DMA((5, n * PIECES)), pltpu.SemaphoreType.DMA((n * PIECES,)),
         ] + [room(*shape) for shape in slots]
-        + [pltpu.SemaphoreType.DMA((count,)) for count in counts],
+        + [pltpu.SemaphoreType.DMA((count * PIECES,)) for count in counts],
         compiler_params=pltpu.CompilerParams(
             collective_id=2, has_side_effects=True, vmem_limit_bytes=60 * 2**20
         ),
@@ -440,7 +465,7 @@
         out_shape=jax.ShapeDtypeStruct((n,) + own.shape, own.dtype),
         in_specs=[pl.BlockSpec(memory_space=pltpu.VMEM)],
         out_specs=pl.BlockSpec(memory_space=pltpu.VMEM),
-        scratch_shapes=[pltpu.SemaphoreType.DMA((5, n)), pltpu.SemaphoreType.DMA((n,))],
+        scratch_shapes=[pltpu.SemaphoreType.DMA((5, n * PIECES)), pltpu.SemaphoreType.DMA((n * PIECES,))],
         compiler_params=pltpu.CompilerParams(
             collective_id=0, has_side_effects=True, vmem_limit_bytes=60 * 2**20
         ),
@@ -464,7 +489,7 @@
         scratch_shapes=[
             room(n // 2), room(2 * lines), room(lines), room(lines), room(lines),
             room(2 * lines), room(lines), room(lines),
-        ] + [pltpu.SemaphoreType.DMA((count,)) for count in counts],
+        ] + [pltpu.SemaphoreType.DMA((count * PIECES,)) for count in counts],
         compiler_params=pltpu.CompilerParams(
             collective_id=1, has_side_effects=True, vmem_limit_bytes=60 * 2**20
         ),

time: 75 us -> 75.6 us (level)
  Pallas kernels: 69.1 us -> 70.4 us
    pallas_call x1, Pallas kernels: 69.1 us -> 70.4 us  [fused(): pl.pallas_call(functools.partial(fused_kernel, n), out_shape=jax.ShapeDty...]
where the time goes in v4:
time: 75.6 us; the launch traced here: 75.3 us
  Pallas kernels  70.4 us (93%)
  other arithmetic  3.3 us (4%)
  local copies, waits for them, and re-layouts  1.57 us (2%)
    pallas_call x1, Pallas kernels, fused(): pl.pallas_call(functools.partial(fused_kernel, n), out_shape=jax.ShapeDty...  70.4 us
    unnamed x1, local copies, waits for them, and re-layouts  1.57 us
    concatenate x1, other arithmetic, shards(): jnp.concatenate([hidden_rows.reshape(block_rows, feature_count), tail], a...  1.56 us

profile of v4, /device:TPU:8, one launch (start us, length us, event | category | flops | bytes accessed | tf_op | source)
XLA Modules:
  0.0 75.3 jit_solution(16754313401434070750)
XLA Ops:
  0.0 0.9 %multiply_divide_fusion = f32[2,8,8]{2,1,0:T(8,128)S(1)} fusion(s32[2,8,8]{2,1,0:T(8,128)} %param.8), kind=kOutput, calls=%fused_computation.9 | output fusion | flops 535 | bytes 1024 | tf_op jit(solution)/shard_map/div | solution.py:502
  0.9 0.8 %select_reduce_fusion = f32[2,8,16]{2,1,0:T(8,128)S(1)} fusion(f32[2,8,8]{2,1,0:T(8,128)S(1)} %multiply_divide_fusion, s32[2,8,8]{2,1,0:T(8,128)} %param.7), kind=kLoop, calls=%fused_computation.1 | loop fusion | flops 5888 | bytes 2048 | tf_op jit(solution)/shard_map/reduce_sum | solution.py:504
  1.7 0.1 fusion.4
  1.8 1.6 %pad_maximum_fusion.own_ref = bf16[16,4224]{1,0:T(8,128)(2,1)} fusion(bf16[16,128]{1,0:T(8,128)(2,1)S(1)} %fusion.4, bf16[16,4096]{1,0:T(8,128)(2,1)} %bitcast.6), kind=kLoop, calls=%fused_computation | loop fusion | flops 270336 | bytes 270336 | tf_op jit(solution)/shard_map/concatenate | solution.py:518
  3.3 70.4 %fused.1 = bf16[16,4096]{1,0:T(8,128)(2,1)} custom-call(bf16[16,4224]{1,0:T(8,128)(2,1)} %pad_maximum_fusion.own_ref, bf16[4096,512]{1,0:T(8,128)(2,1)} %gate_hbm.1, bf16[4096,512]{1,0:T(8,128)(2,1)} %up_hbm.1, bf16[512,4096]{1,0:T(8,128)(2,1)} %down_hbm.1), custom_call_target="tpu_custom_call" | custom-call | tf_op jit(solution)/shard_map/fused/pallas_call | solution.py:444
  73.7 1.6 %copy.8 = bf16[2,8,4096]{2,1,0:T(8,128)(2,1)} copy(bf16[2,8,4096]{2,1,0:T(8,128)(2,1)} %bitcast.5) | data formatting | bytes 262144
  (1 shorter events, 0.0 us)

commit v5 on v4

--- a/solution.py
+++ b/solution.py
@@ -10,7 +10,7 @@
 
 route_scale = 2.5
 LANES = 128
-PIECES = 2
+PIECES = 1
 
 
 def span(piece, size):
@@ -160,9 +160,10 @@
         side_step(near, k - 1, True, True)
     for k in range(lines):
         side_step(far, k, False, True)
-    work_on(me, near, far)
+    work_on(me, near)
     for k in range(lines):
         side_step(both, k, False, True)
+    work_on(far)
     if between is not None:
         between()
     work_on(both)

time: 75.6 us -> 72.5 us (0.959)
  Pallas kernels: 70.4 us -> 67.3 us
    pallas_call x1, Pallas kernels: 70.4 us -> 67.3 us  [fused(): pl.pallas_call(functools.partial(fused_kernel, n), out_shape=jax.ShapeDty...]
where the time goes in v5:
time: 72.5 us; the launch traced here: 72.2 us
  Pallas kernels  67.3 us (93%)
  other arithmetic  3.3 us (5%)
  local copies, waits for them, and re-layouts  1.57 us (2%)
    pallas_call x1, Pallas kernels, fused(): pl.pallas_call(functools.partial(fused_kernel, n), out_shape=jax.ShapeDty...  67.3 us
    unnamed x1, local copies, waits for them, and re-layouts  1.57 us
    concatenate x1, other arithmetic, shards(): jnp.concatenate([hidden_rows.reshape(block_rows, feature_count), tail], a...  1.56 us

profile of v5, /device:TPU:8, one launch (start us, length us, event | category | flops | bytes accessed | tf_op | source)
XLA Modules:
  0.0 72.2 jit_solution(6005513208419398420)
XLA Ops:
  0.0 0.9 %multiply_divide_fusion = f32[2,8,8]{2,1,0:T(8,128)S(1)} fusion(s32[2,8,8]{2,1,0:T(8,128)} %param.8), kind=kOutput, calls=%fused_computation.9 | output fusion | flops 535 | bytes 1024 | tf_op jit(solution)/shard_map/div | solution.py:503
  0.9 0.8 %select_reduce_fusion = f32[2,8,16]{2,1,0:T(8,128)S(1)} fusion(f32[2,8,8]{2,1,0:T(8,128)S(1)} %multiply_divide_fusion, s32[2,8,8]{2,1,0:T(8,128)} %param.7), kind=kLoop, calls=%fused_computation.1 | loop fusion | flops 5888 | bytes 2048 | tf_op jit(solution)/shard_map/reduce_sum | solution.py:505
  1.7 0.1 fusion.4
  1.8 1.6 %pad_maximum_fusion.own_ref = bf16[16,4224]{1,0:T(8,128)(2,1)} fusion(bf16[16,128]{1,0:T(8,128)(2,1)S(1)} %fusion.4, bf16[16,4096]{1,0:T(8,128)(2,1)} %bitcast.6), kind=kLoop, calls=%fused_computation | loop fusion | flops 270336 | bytes 270336 | tf_op jit(solution)/shard_map/concatenate | solution.py:519
  3.3 67.3 %fused.1 = bf16[16,4096]{1,0:T(8,128)(2,1)} custom-call(bf16[16,4224]{1,0:T(8,128)(2,1)} %pad_maximum_fusion.own_ref, bf16[4096,512]{1,0:T(8,128)(2,1)} %gate_hbm.1, bf16[4096,512]{1,0:T(8,128)(2,1)} %up_hbm.1, bf16[512,4096]{1,0:T(8,128)(2,1)} %down_hbm.1), custom_call_target="tpu_custom_call" | custom-call | tf_op jit(solution)/shard_map/fused/pallas_call | solution.py:445
  70.6 1.6 %copy.8 = bf16[2,8,4096]{2,1,0:T(8,128)(2,1)} copy(bf16[2,8,4096]{2,1,0:T(8,128)(2,1)} %bitcast.5) | data formatting | bytes 262144
  (1 shorter events, 0.0 us)

commit v6 on v5

--- a/solution.py
+++ b/solution.py
@@ -399,7 +399,7 @@
             )
             act_ref[:total, columns] = (gate / (1.0 + jnp.exp(-gate)) * up).astype(jnp.bfloat16)
 
-        wide = min(features, 4 * LANES)
+        wide = min(features, 8 * LANES)
 
         @pl.loop(0, features // wide)
         def _(tile):

time: 72.5 us -> 71.6 us (0.988)
  Pallas kernels: 67.3 us -> 66.4 us
    pallas_call x1, Pallas kernels: 67.3 us -> 66.4 us  [fused(): pl.pallas_call(functools.partial(fused_kernel, n), out_shape=jax.ShapeDty...]
where the time goes in v6:
time: 71.6 us; the launch traced here: 71.3 us
  Pallas kernels  66.4 us (93%)
  other arithmetic  3.3 us (5%)
  local copies, waits for them, and re-layouts  1.57 us (2%)
    pallas_call x1, Pallas kernels, fused(): pl.pallas_call(functools.partial(fused_kernel, n), out_shape=jax.ShapeDty...  66.4 us
    unnamed x1, local copies, waits for them, and re-layouts  1.57 us
    concatenate x1, other arithmetic, shards(): jnp.concatenate([hidden_rows.reshape(block_rows, feature_count), tail], a...  1.56 us

profile of v6, /device:TPU:8, one launch (start us, length us, event | category | flops | bytes accessed | tf_op | source)
XLA Modules:
  0.0 71.3 jit_solution(5343228269729442841)
XLA Ops:
  0.0 0.9 %multiply_divide_fusion = f32[2,8,8]{2,1,0:T(8,128)S(1)} fusion(s32[2,8,8]{2,1,0:T(8,128)} %param.8), kind=kOutput, calls=%fused_computation.9 | output fusion | flops 535 | bytes 1024 | tf_op jit(solution)/shard_map/div | solution.py:503
  0.9 0.8 %select_reduce_fusion = f32[2,8,16]{2,1,0:T(8,128)S(1)} fusion(f32[2,8,8]{2,1,0:T(8,128)S(1)} %multiply_divide_fusion, s32[2,8,8]{2,1,0:T(8,128)} %param.7), kind=kLoop, calls=%fused_computation.1 | loop fusion | flops 5888 | bytes 2048 | tf_op jit(solution)/shard_map/reduce_sum | solution.py:505
  1.7 0.1 fusion.4
  1.8 1.6 %pad_maximum_fusion.own_ref = bf16[16,4224]{1,0:T(8,128)(2,1)} fusion(bf16[16,128]{1,0:T(8,128)(2,1)S(1)} %fusion.4, bf16[16,4096]{1,0:T(8,128)(2,1)} %bitcast.6), kind=kLoop, calls=%fused_computation | loop fusion | flops 270336 | bytes 270336 | tf_op jit(solution)/shard_map/concatenate | solution.py:519
  3.3 66.4 %fused.1 = bf16[16,4096]{1,0:T(8,128)(2,1)} custom-call(bf16[16,4224]{1,0:T(8,128)(2,1)} %pad_maximum_fusion.own_ref, bf16[4096,512]{1,0:T(8,128)(2,1)} %gate_hbm.1, bf16[4096,512]{1,0:T(8,128)(2,1)} %up_hbm.1, bf16[512,4096]{1,0:T(8,128)(2,1)} %down_hbm.1), custom_call_target="tpu_custom_call" | custom-call | tf_op jit(solution)/shard_map/fused/pallas_call | solution.py:445
  69.7 1.6 %copy.8 = bf16[2,8,4096]{2,1,0:T(8,128)(2,1)} copy(bf16[2,8,4096]{2,1,0:T(8,128)(2,1)} %bitcast.5) | data formatting | bytes 262144
  (1 shorter events, 0.0 us)
